TPU v7x, 256 devices: a whole 4x4x8 slice. The times are simulated.
256 devices in a mesh: ctx: 64 (over x, y_lo, z), rep: 4 (over y_hi, core).
Axes of the slice: x: 4, y: 4 (y_hi: 2, y_lo: 2; y = y_hi * 2 + y_lo), z: 8, core: 2. Of those that a mesh axis runs over, the one named last changes fastest.
Arguments:
- tokens: bfloat16 [4, 8192, 2880], P('rep', 'ctx'), may hold values from -6 to 6
- router_w: bfloat16 [2880, 32], replicated, may hold values from -0.109375 to 0.109375
- router_b: float32 [32], replicated, may hold values from -4 to 4
- hidden: bfloat16 [4, 8192, 4, 1536], P('rep', 'ctx'), may hold values from -6 to 6
- teacher_idx: int32 [4, 8192, 4], P('rep', 'ctx'), may hold values from 0 to 31, all different within a row
- merge_map: int32 [32], replicated, may hold values from 0 to 15, as said below
- merge_coef: float32 [32], replicated, may hold values from 0.3 to 1.5
- source_w: bfloat16 [32, 1536, 1536], P(None, 'ctx'), may hold values from -0.15625 to 0.15625
- out_grad: bfloat16 [4, 8192, 1536], P('rep', 'ctx'), may hold values from -6 to 6
Outputs:
- mixed: bfloat16 [4, 8192, 1536], P('rep', 'ctx')
- hidden_grad: bfloat16 [4, 8192, 4, 1536], P('rep', 'ctx')
- token_grad: bfloat16 [4, 8192, 2880], P('rep', 'ctx')
- router_w_grad: float32 [2880, 32], replicated
- router_b_grad: float32 [32], replicated
- coef_grad: float32 [32], replicated
- source_w_grad: float32 [32, 1536, 1536], P(None, 'ctx', 'rep')
Inputs may be any that keep to these rules, and one draw needn't show every extreme that they name: `teacher_idx`: each token names 4 different experts. `merge_map`: each of the 16 combinations takes exactly two of the 32 experts.
All inputs are finite; a program needn't handle non-finite values.
Results may differ from a plain program's by a relative error of at most 0.0064.
Values may be sent and summed in bfloat16 or wider, within the bound.
A program may use at most 128 MiB of HBM per device.

v0:
```python
import math
import jax
import jax.numpy as jnp
from jax import lax
from jax.sharding import PartitionSpec as P

MERGED = 16


def expert_rows(rows_hidden, rows_grad, rows_member, lane_weights):
    row_count = rows_hidden.shape[0]
    out_rows = jnp.zeros((row_count, lane_weights.shape[1]), jnp.float32)
    back_rows = jnp.zeros((row_count, lane_weights.shape[2]), jnp.float32)
    weight = lane_weights[0]
    selected = (rows_member == 0)[:, None]
    forward = lax.dot_general(
        rows_hidden, weight, (((1,), (1,)), ((), ())), preferred_element_type=jnp.float32
    )
    out_rows = jnp.where(selected, forward, out_rows)
    backward = jnp.dot(rows_grad, weight, preferred_element_type=jnp.float32)
    back_rows = jnp.where(selected, backward, back_rows)
    masked = jnp.where(selected, rows_grad, jnp.zeros_like(rows_grad))
    grad_list = [
        lax.dot_general(
            masked, rows_hidden, (((0,), (0,)), ((), ())), preferred_element_type=jnp.float32
        )
    ]
    return (out_rows, back_rows, jnp.stack(grad_list))


def on_device(
    tokens, router_w, router_b, hidden, teacher_idx, merge_map, merge_coef, source_w, out_grad
):
    ctx_count = lax.axis_size("ctx")
    rep_count = lax.axis_size("rep")
    tok_count = tokens.shape[1]
    feature_count = tokens.shape[2]
    top_count = teacher_idx.shape[2]
    hidden_width = hidden.shape[3]
    out_width = out_grad.shape[2]
    source_count = router_w.shape[1]
    row_share = source_w.shape[1]
    per_lane = max(1, MERGED // ctx_count)
    copies = max(1, ctx_count // MERGED)
    capacity = 5 * tok_count * top_count // (4 * ctx_count)
    slot_count = tok_count * top_count
    grad_scale = 1.0 / math.sqrt(tok_count * ctx_count * rep_count)
    flat_x = tokens.reshape(tok_count, feature_count)
    logits = jnp.dot(flat_x, router_w, preferred_element_type=jnp.float32) + router_b
    choice_ids = teacher_idx.reshape(tok_count, top_count)
    pick_table = choice_ids[:, :, None] == jnp.arange(source_count, dtype=jnp.int32)[None, None, :]
    pick_float = pick_table.astype(jnp.float32)
    chosen = jnp.sum(pick_float * logits[:, None, :], axis=2)
    raised = jnp.exp(chosen)
    gate_probs = raised / jnp.sum(raised, axis=1, keepdims=True)
    merged_id = jnp.sum(jnp.where(pick_table, merge_map[None, None, :], 0), axis=2)
    position = lax.axis_index("ctx") * tok_count + jnp.arange(tok_count, dtype=jnp.int32)
    lane_id = merged_id // per_lane * copies + (position % copies)[:, None]
    member_id = (merged_id % per_lane).reshape(-1)
    lane_flat = lane_id.reshape(-1)
    onehot = (lane_flat[:, None] == jnp.arange(ctx_count, dtype=jnp.int32)[None, :]).astype(
        jnp.int32
    )
    before = jnp.cumsum(onehot, axis=0) - onehot
    slot_rank = jnp.sum(before * onehot, axis=1)
    is_kept = slot_rank < capacity
    slot_index = jnp.where(is_kept, lane_flat * capacity + slot_rank, ctx_count * capacity)
    slot_source = (
        jnp.full((ctx_count * capacity + 1,), slot_count, jnp.int32)
        .at[slot_index]
        .set(jnp.arange(slot_count, dtype=jnp.int32))[: ctx_count * capacity]
    )
    slot_grad = (gate_probs[:, :, None] * out_grad.reshape(tok_count, 1, out_width)).astype(
        jnp.bfloat16
    )
    pad_hidden = jnp.concatenate(
        [hidden.reshape(slot_count, hidden_width), jnp.zeros((1, hidden_width), jnp.bfloat16)],
        axis=0,
    )
    pad_grad = jnp.concatenate(
        [slot_grad.reshape(slot_count, out_width), jnp.zeros((1, out_width), jnp.bfloat16)], axis=0
    )
    pad_member = jnp.concatenate([member_id, jnp.zeros((1,), jnp.int32)], axis=0)
    send_hidden = pad_hidden[slot_source].reshape(ctx_count, capacity, hidden_width)
    send_grad = pad_grad[slot_source].reshape(ctx_count, capacity, out_width)
    send_member = pad_member[slot_source].reshape(ctx_count, capacity)
    lane_group = lax.axis_index("ctx") // copies
    same_group = merge_map[:, None] == merge_map[None, :]
    earlier = jnp.arange(source_count)[:, None] > jnp.arange(source_count)[None, :]
    member_rank = jnp.sum((same_group & earlier).astype(jnp.int32), axis=1)
    source_order = (
        jnp.zeros((source_count,), jnp.int32)
        .at[2 * merge_map + member_rank]
        .set(jnp.arange(source_count, dtype=jnp.int32))
    )
    picked = source_w[source_order].reshape(
        MERGED // per_lane, 2 * per_lane, row_share, hidden_width
    )
    outgoing = jnp.repeat(picked, copies, axis=0)
    arrived = lax.all_to_all(outgoing, "ctx", split_axis=0, concat_axis=2, tiled=True)
    coef_table = merge_coef[source_order].reshape(MERGED // per_lane, per_lane, 2)
    pair_coef = lax.dynamic_index_in_dim(coef_table, lane_group, 0, keepdims=False)
    lane_weights = (
        pair_coef[:, 0, None, None] * arrived[:, 0].astype(jnp.float32)
        + pair_coef[:, 1, None, None] * arrived[:, 1].astype(jnp.float32)
    ).astype(jnp.bfloat16)
    recv_hidden, recv_grad, recv_member = (
        lax.all_to_all(send_hidden, "ctx", split_axis=0, concat_axis=0, tiled=True),
        lax.all_to_all(send_grad, "ctx", split_axis=0, concat_axis=0, tiled=True),
        lax.all_to_all(send_member, "ctx", split_axis=0, concat_axis=0, tiled=True),
    )
    out_rows, back_rows, lane_grads = expert_rows(
        recv_hidden.reshape(-1, hidden_width),
        recv_grad.reshape(-1, out_width),
        recv_member.reshape(-1),
        lane_weights,
    )
    home_out, home_back = (
        lax.all_to_all(
            out_rows.astype(jnp.bfloat16).reshape(ctx_count, capacity, out_width),
            "ctx",
            split_axis=0,
            concat_axis=0,
            tiled=True,
        ),
        lax.all_to_all(
            back_rows.astype(jnp.bfloat16).reshape(ctx_count, capacity, hidden_width),
            "ctx",
            split_axis=0,
            concat_axis=0,
            tiled=True,
        ),
    )
    slot_out = jnp.concatenate(
        [home_out.reshape(-1, out_width), jnp.zeros((1, out_width), jnp.bfloat16)], axis=0
    )[slot_index].reshape(tok_count, top_count, out_width)
    hidden_grad = jnp.concatenate(
        [home_back.reshape(-1, hidden_width), jnp.zeros((1, hidden_width), jnp.bfloat16)], axis=0
    )[slot_index].reshape(1, tok_count, top_count, hidden_width)
    mixed = (
        jnp.sum(gate_probs[:, :, None] * slot_out.astype(jnp.float32), axis=1)
        .astype(jnp.bfloat16)
        .reshape(1, tok_count, out_width)
    )
    score_grad = jnp.einsum(
        "td,tkd->tk",
        out_grad.reshape(tok_count, out_width),
        slot_out,
        preferred_element_type=jnp.float32,
    )
    chosen_grad = gate_probs * (
        score_grad - jnp.sum(gate_probs * score_grad, axis=1, keepdims=True)
    )
    logit_grad = jnp.sum(pick_float * chosen_grad[:, :, None], axis=1)
    logit_half = logit_grad.astype(jnp.bfloat16)
    token_grad = (
        lax.dot_general(
            logit_half, router_w, (((1,), (1,)), ((), ())), preferred_element_type=jnp.float32
        )
        .astype(jnp.bfloat16)
        .reshape(1, tok_count, feature_count)
    )
    part_router_w = lax.dot_general(
        flat_x, logit_half, (((0,), (0,)), ((), ())), preferred_element_type=jnp.float32
    )
    part_router_b = jnp.sum(logit_grad, axis=0)
    arrived_grads = lax.all_to_all(
        lane_grads.reshape(per_lane, ctx_count, row_share, hidden_width),
        "ctx",
        split_axis=1,
        concat_axis=0,
        tiled=True,
    )
    merged_grad = (
        arrived_grads.reshape(MERGED // per_lane, copies, per_lane, row_share, hidden_width)
        .sum(axis=1)
        .reshape(MERGED, row_share, hidden_width)
    )
    source_grad = merged_grad[merge_map]
    coef_part = jnp.einsum(
        "edf,edf->e", source_grad, source_w.astype(jnp.float32), precision=lax.Precision.HIGHEST
    )
    summed = lax.psum_scatter(
        source_grad * merge_coef[:, None, None], "rep", scatter_dimension=2, tiled=True
    )
    source_w_grad = summed * grad_scale
    router_sum, bias_sum, coef_sum = lax.psum(
        (part_router_w, part_router_b, coef_part), ("ctx", "rep")
    )
    return (
        mixed,
        hidden_grad,
        token_grad,
        router_sum * grad_scale,
        bias_sum * grad_scale,
        coef_sum * grad_scale,
        source_w_grad,
    )


def solution(mesh):
    in_specs = (
        P("rep", "ctx", None),
        P(),
        P(),
        P("rep", "ctx", None, None),
        P("rep", "ctx", None),
        P(),
        P(),
        P(None, "ctx", None),
        P("rep", "ctx", None),
    )
    out_specs = (
        P("rep", "ctx", None),
        P("rep", "ctx", None, None),
        P("rep", "ctx", None),
        P(),
        P(),
        P(),
        P(None, "ctx", "rep"),
    )
    return jax.shard_map(
        on_device, mesh=mesh, in_specs=in_specs, out_specs=out_specs, check_vma=False
    )
```

profile of v0, /device:TPU:1, one launch (start us, length us, event | category | flops | bytes accessed | tf_op | source)
XLA Modules:
  0.0 1014.5 jit_solution(12828136133311541424)
XLA Ops:
  17.5 13.5 %all-to-all-start = ((s32[64,1,10]{2,1,0:T(1,128)}), s32[64,1,10]{2,1,0:T(1,128)S(1)}, u32[]{:S(2)}, u32[]{:S(2)}) async-start(s32[64,1,10]{2,1,0:T(1,128)} %bitcast.5), calls=%async_computation | async-start | bytes 65536 | tf_op jit(solution)/shard_map/all_to_all | solution.py:110
  37.5 4.2 reshape.274
  41.7 11.1 %all-to-all-start.1 = ((bf16[64,10,1536]{2,1,0:T(8,128)(2,1)}), bf16[64,10,1536]{2,1,0:T(8,128)(2,1)}, u32[]{:S(2)}, u32[]{:S(2)}) async-start(bf16[64,10,1536]{2,1,0:T(8,128)(2,1)} %reshape.274), calls=%async_computation.1 | async-start | bytes 6291456 | tf_op jit(solution)/shard_map/all_to_all | solution.py:108
  55.8 66.0 %all-to-all-done.1 = bf16[64,10,1536]{2,1,0:T(8,128)(2,1)} async-done(((bf16[64,10,1536]{2,1,0:T(8,128)(2,1)}), bf16[64,10,1536]{2,1,0:T(8,128)(2,1)}, u32[]{:S(2)}, u32[]{:S(2)}) %all-to-all-start.1) | async-done | bytes 1966112 | tf_op jit(solution)/shard_map/all_to_all | solution.py:108
  121.8 6.5 broadcast_in_dim.85
  128.3 10.5 %all-to-all-start.2 = ((bf16[64,2,24,1536]{3,2,1,0:T(8,128)(2,1)}), bf16[64,2,24,1536]{3,2,1,0:T(8,128)(2,1)}, u32[]{:S(2)}, u32[]{:S(2)}) async-start(bf16[64,2,24,1536]{3,2,1,0:T(8,128)(2,1)} %bitcast.77), calls=%async_computation.2 | async-start | bytes 18874368 | tf_op jit(solution)/shard_map/all_to_all | solution.py:100
  143.4 199.7 %all-to-all-done.2 = bf16[64,2,24,1536]{3,2,1,0:T(8,128)(2,1)} async-done(((bf16[64,2,24,1536]{3,2,1,0:T(8,128)(2,1)}), bf16[64,2,24,1536]{3,2,1,0:T(8,128)(2,1)}, u32[]{:S(2)}, u32[]{:S(2)}) %all-to-all-start.2) | async-done | bytes 9437216 | tf_op jit(solution)/shard_map/all_to_all | solution.py:100
  343.1 8.1 copy.44
  351.1 9.8 select_convert_fusion.1
  360.9 4.2 reshape.279
  365.1 11.4 %all-to-all-start.3 = ((bf16[64,10,1536]{2,1,0:T(8,128)(2,1)}), bf16[64,10,1536]{2,1,0:T(8,128)(2,1)}, u32[]{:S(2)}, u32[]{:S(2)}) async-start(bf16[64,10,1536]{2,1,0:T(8,128)(2,1)} %reshape.279), calls=%async_computation.3 | async-start | bytes 6291456 | tf_op jit(solution)/shard_map/all_to_all | solution.py:119
  378.9 5.0 mul.171
  384.2 61.5 %all-to-all-done.3 = bf16[64,10,1536]{2,1,0:T(8,128)(2,1)} async-done(((bf16[64,10,1536]{2,1,0:T(8,128)(2,1)}), bf16[64,10,1536]{2,1,0:T(8,128)(2,1)}, u32[]{:S(2)}, u32[]{:S(2)}) %all-to-all-start.3) | async-done | bytes 1966112 | tf_op jit(solution)/shard_map/all_to_all | solution.py:119
  445.7 4.3 reshape.280
  461.9 3.7 gather_fusion.5
  465.7 4.2 reshape.283
  469.9 11.0 %all-to-all-start.4 = ((bf16[64,10,1536]{2,1,0:T(8,128)(2,1)}), bf16[64,10,1536]{2,1,0:T(8,128)(2,1)}, u32[]{:S(2)}, u32[]{:S(2)}) async-start(bf16[64,10,1536]{2,1,0:T(8,128)(2,1)} %reshape.283), calls=%async_computation.4 | async-start | bytes 6291456 | tf_op jit(solution)/shard_map/all_to_all | solution.py:109
  480.8 4.2 reshape.380
  485.1 64.7 %all-to-all-done.4 = bf16[64,10,1536]{2,1,0:T(8,128)(2,1)} async-done(((bf16[64,10,1536]{2,1,0:T(8,128)(2,1)}), bf16[64,10,1536]{2,1,0:T(8,128)(2,1)}, u32[]{:S(2)}, u32[]{:S(2)}) %all-to-all-start.4) | async-done | bytes 1966112 | tf_op jit(solution)/shard_map/all_to_all | solution.py:109
  554.5 4.0 copy.46
  558.4 9.7 convolution_bitcast_fusion
  568.1 10.7 %all-to-all-start.6 = ((f32[1,64,24,1536]{3,2,0,1:T(8,128)}), f32[1,64,24,1536]{3,2,0,1:T(8,128)}, u32[]{:S(2)}, u32[]{:S(2)}) async-start(f32[1,64,24,1536]{3,2,0,1:T(8,128)} %convolution_bitcast_fusion), calls=%async_computation.6 | async-start | bytes 18874368 | tf_op jit(solution)/shard_map/all_to_all | solution.py:167
  580.2 205.3 %all-to-all-done.6 = f32[1,64,24,1536]{3,2,0,1:T(8,128)} async-done(((f32[1,64,24,1536]{3,2,0,1:T(8,128)}), f32[1,64,24,1536]{3,2,0,1:T(8,128)}, u32[]{:S(2)}, u32[]{:S(2)}) %all-to-all-start.6) | async-done | bytes 9437216 | tf_op jit(solution)/shard_map/all_to_all | solution.py:167
  785.5 5.2 reduce_sum.102
  793.8 6.3 broadcast_multiply_fusion
  801.6 9.6 select_convert_fusion
  811.3 4.2 reshape.285
  815.5 12.3 %all-to-all-start.5 = ((bf16[64,10,1536]{2,1,0:T(8,128)(2,1)}), bf16[64,10,1536]{2,1,0:T(8,128)(2,1)}, u32[]{:S(2)}, u32[]{:S(2)}) async-start(bf16[64,10,1536]{2,1,0:T(8,128)(2,1)} %reshape.285), calls=%async_computation.5 | async-start | bytes 6291456 | tf_op jit(solution)/shard_map/all_to_all | solution.py:126
  832.1 81.9 %all-reduce.7.cloned.1.call-done = f32[2880,32]{0,1:T(8,128)} async-done(((f32[2880,32]{0,1:T(8,128)}), f32[2880,32]{0,1:T(8,128)}) %all-reduce.7.cloned.1.call-update) | async-done | bytes 368656 | tf_op jit(solution)/shard_map/psum | solution.py:187
  915.8 4.2 reshape.286
  924.7 3.8 reshape.287
  928.5 75.4 %all-reduce.4 = (f32[32]{0:T(128)S(1)}, f32[32]{0:T(128)S(1)}) all-reduce(f32[32]{0:T(128)S(1)} %get-tuple-element.7, f32[32]{0:T(128)S(1)} %get-tuple-element.16), channel_id=1, replica_groups=mesh['ctx'=64,'rep'=4] {'ctx','rep'}, use_global_device_ids=true, to_apply=%region_14.15 | all-reduce | flops 64 | bytes 512 | tf_op jit(solution)/shard_map/psum | solution.py:187
  (109 shorter events, 62.2 us)
Async XLA Ops:
  8.0 375.8 %copy-start = (bf16[1,128,2880]{1,2,0:T(8,128)(2,1)S(1)}, bf16[1,128,2880]{1,2,0:T(8,128)(2,1)}, u32[]{:S(2)}) copy-start(bf16[1,128,2880]{1,2,0:T(8,128)(2,1)} %param.9) | copy-start | bytes 2211844
  10.8 20.2 %copy-start.7 = (bf16[1,128,4,1536]{3,2,1,0:T(4,128)(2,1)S(1)}, bf16[1,128,4,1536]{3,2,1,0:T(4,128)(2,1)}, u32[]{:S(2)}) copy-start(bf16[1,128,4,1536]{3,2,1,0:T(4,128)(2,1)} %param.12) | copy-start | bytes 4718596
  17.5 24.2 %all-to-all-start = ((s32[64,1,10]{2,1,0:T(1,128)}), s32[64,1,10]{2,1,0:T(1,128)S(1)}, u32[]{:S(2)}, u32[]{:S(2)}) async-start(s32[64,1,10]{2,1,0:T(1,128)} %bitcast.5), calls=%async_computation | async-start | bytes 65536 | tf_op jit(solution)/shard_map/all_to_all | solution.py:110
  41.7 11.1 %copy-start.12 = (s32[32]{0:T(128)S(1)}, s32[32]{0:T(128)}, u32[]{:S(2)}) copy-start(s32[32]{0:T(128)} %param.14) | copy-start | bytes 388
  41.7 12.0 %copy-start.2 = (bf16[32,24,1536]{2,1,0:T(8,128)(2,1)S(1)}, bf16[32,24,1536]{2,1,0:T(8,128)(2,1)}, u32[]{:S(2)}) copy-start(bf16[32,24,1536]{2,1,0:T(8,128)(2,1)} %param.16) | copy-start | bytes 7077892
  41.7 80.1 %all-to-all-start.1 = ((bf16[64,10,1536]{2,1,0:T(8,128)(2,1)}), bf16[64,10,1536]{2,1,0:T(8,128)(2,1)}, u32[]{:S(2)}, u32[]{:S(2)}) async-start(bf16[64,10,1536]{2,1,0:T(8,128)(2,1)} %reshape.274), calls=%async_computation.1 | async-start | bytes 6291456 | tf_op jit(solution)/shard_map/all_to_all | solution.py:108
  128.3 10.5 %copy-start.1 = (f32[32]{0:T(128)S(1)}, f32[32]{0:T(128)}, u32[]{:S(2)}) copy-start(f32[32]{0:T(128)} %param.15) | copy-start | bytes 388
  128.3 214.8 %all-to-all-start.2 = ((bf16[64,2,24,1536]{3,2,1,0:T(8,128)(2,1)}), bf16[64,2,24,1536]{3,2,1,0:T(8,128)(2,1)}, u32[]{:S(2)}, u32[]{:S(2)}) async-start(bf16[64,2,24,1536]{3,2,1,0:T(8,128)(2,1)} %bitcast.77), calls=%async_computation.2 | async-start | bytes 18874368 | tf_op jit(solution)/shard_map/all_to_all | solution.py:100
  365.1 11.4 %copy-start.9 = (bf16[1,128,1536]{2,1,0:T(8,128)(2,1)S(1)}, bf16[1,128,1536]{2,1,0:T(8,128)(2,1)}, u32[]{:S(2)}) copy-start(bf16[1,128,1536]{2,1,0:T(8,128)(2,1)} %param.17) | copy-start | bytes 1179652
  365.1 80.5 %all-to-all-start.3 = ((bf16[64,10,1536]{2,1,0:T(8,128)(2,1)}), bf16[64,10,1536]{2,1,0:T(8,128)(2,1)}, u32[]{:S(2)}, u32[]{:S(2)}) async-start(bf16[64,10,1536]{2,1,0:T(8,128)(2,1)} %reshape.279), calls=%async_computation.3 | async-start | bytes 6291456 | tf_op jit(solution)/shard_map/all_to_all | solution.py:119
  378.9 5.0 copy-start.8
  378.9 5.0 copy-start.13
  378.9 5.2 copy-start.11
  454.6 3.0 copy-start.10
  457.5 1.8 copy-start.5
  469.9 80.0 %all-to-all-start.4 = ((bf16[64,10,1536]{2,1,0:T(8,128)(2,1)}), bf16[64,10,1536]{2,1,0:T(8,128)(2,1)}, u32[]{:S(2)}, u32[]{:S(2)}) async-start(bf16[64,10,1536]{2,1,0:T(8,128)(2,1)} %reshape.283), calls=%async_computation.4 | async-start | bytes 6291456 | tf_op jit(solution)/shard_map/all_to_all | solution.py:109
  552.7 5.7 copy-start.3
  568.1 217.4 %all-to-all-start.6 = ((f32[1,64,24,1536]{3,2,0,1:T(8,128)}), f32[1,64,24,1536]{3,2,0,1:T(8,128)}, u32[]{:S(2)}, u32[]{:S(2)}) async-start(f32[1,64,24,1536]{3,2,0,1:T(8,128)} %convolution_bitcast_fusion), calls=%async_computation.6 | async-start | bytes 18874368 | tf_op jit(solution)/shard_map/all_to_all | solution.py:167
  578.9 335.2 %all-reduce.7.cloned.1.call-start = ((), (), s32[]{:S(2)}) async-start(), calls=%async_computation.8 | async-start | bytes 753664 | tf_op jit(solution)/shard_map/psum | solution.py:187
  580.2 424.2 %reduce-scatter.2.cloned.1.call-start = ((), (), s32[]{:S(2)}) async-start(), calls=%async_computation.9 | async-start | bytes 5898240 | tf_op jit(solution)/shard_map/reduce_scatter | solution.py:183
  800.1 1.5 copy-start.4
  815.5 13.6 %copy-start.6 = (bf16[128,4,1536]{2,1,0:T(4,128)(2,1)S(1)}, bf16[128,4,1536]{2,1,0:T(4,128)(2,1)}, u32[]{:S(2)}) copy-start(bf16[128,4,1536]{2,1,0:T(4,128)(2,1)} %copy-done.5) | copy-start | bytes 4718596
  815.5 100.3 %all-to-all-start.5 = ((bf16[64,10,1536]{2,1,0:T(8,128)(2,1)}), bf16[64,10,1536]{2,1,0:T(8,128)(2,1)}, u32[]{:S(2)}, u32[]{:S(2)}) async-start(bf16[64,10,1536]{2,1,0:T(8,128)(2,1)} %reshape.285), calls=%async_computation.5 | async-start | bytes 6291456 | tf_op jit(solution)/shard_map/all_to_all | solution.py:126
Sparse Core Ops, SparseCore 0:
  585.8 328.2 all-reduce.6
Sparse Core Ops, SparseCore 1:
  800.2 83.5 reduce-scatter.1
where the time goes:
time: 1020 us; the launch traced here: 1010 us
  waiting for transfers between devices  679 us (67%)
  local copies, waits for them, and re-layouts  104 us (10%)
  starting transfers between devices  80.5 us (8%)
  blocking collectives  75.4 us (7%)
  matrix products  33.5 us (3%)
  other arithmetic  25.9 us (3%)
  between operations  16.1 us (2%)
    all_to_all x1, waiting for transfers between devices, on_device(): lax.all_to_all(lane_grads.reshape(per_lane, ctx_count, row_share, hidden_...  205 us
    all_to_all x1, waiting for transfers between devices, on_device(): lax.all_to_all(outgoing, 'ctx', split_axis=0, concat_axis=2, tiled=True)  200 us
    psum x1, waiting for transfers between devices, on_device(): lax.psum((part_router_w, part_router_b, coef_part), ('ctx', 'rep'))  81.9 us
    psum x1, blocking collectives, on_device(): lax.psum((part_router_w, part_router_b, coef_part), ('ctx', 'rep'))  75.4 us
    all_to_all x1, waiting for transfers between devices, on_device(): lax.all_to_all(send_hidden, 'ctx', split_axis=0, concat_axis=0, tiled=True)  66 us
    all_to_all x1, waiting for transfers between devices, on_device(): lax.all_to_all(send_grad, 'ctx', split_axis=0, concat_axis=0, tiled=True)  64.7 us
    all_to_all x1, waiting for transfers between devices, on_device(): lax.all_to_all(out_rows.astype(jnp.bfloat16).reshape(ctx_count, capacity,...  61.5 us
  transfers between devices with their start and end apart: 9, of which 6 were waited for; matrix products, arithmetic and copies ran while one was open for 8% of the time, Pallas kernels for 0%

commit v1 on v0

--- a/solution.py
+++ b/solution.py
@@ -185,7 +185,7 @@
     )
     source_w_grad = summed * grad_scale
     router_sum, bias_sum, coef_sum = lax.psum(
-        (part_router_w, part_router_b, coef_part), ("ctx", "rep")
+        lax.psum((part_router_w, part_router_b, coef_part), "ctx"), "rep"
     )
     return (
         mixed,

time: 1020 us -> 1440 us (1.41)
  waiting for transfers between devices: 679 us -> 996 us
  blocking collectives: 75.4 us -> 189 us
    psum x1 -> x2, waiting for transfers between devices: 81.9 us -> 604 us  [the longest x1 559 us: on_device(): lax.psum((part_router_w, part_router_b, coef_part), 'ctx')]
    all_to_all x1, waiting for transfers between devices: 205 us -> 0.01 us  [on_device(): lax.all_to_all(lane_grads.reshape(per_lane, ctx_count, row_share, hidden_...]
    psum x1 -> x2, blocking collectives: 75.4 us -> 189 us  [the longest x1 133 us: on_device(): lax.psum((part_router_w, part_router_b, coef_part), 'ctx')]
  transfers between devices with their start and end apart: 9 -> 10, of which waited for: 6 -> 6; matrix products, arithmetic and copies ran while one was open for 8% -> 6% of each run, Pallas kernels for 0% -> 0%
where the time goes in v1:
time: 1440 us
  waiting for transfers between devices  996 us (69%)
  blocking collectives  189 us (13%)
  local copies, waits for them, and re-layouts  104 us (7%)
  starting transfers between devices  74.2 us (5%)
  matrix products  33.5 us (2%)
  other arithmetic  25.9 us (2%)
  between operations  14.4 us (1%)
    psum x1, waiting for transfers between devices, on_device(): lax.psum((part_router_w, part_router_b, coef_part), 'ctx')  559 us
    all_to_all x1, waiting for transfers between devices, on_device(): lax.all_to_all(outgoing, 'ctx', split_axis=0, concat_axis=2, tiled=True)  200 us
    psum x1, blocking collectives, on_device(): lax.psum((part_router_w, part_router_b, coef_part), 'ctx')  133 us
    all_to_all x1, waiting for transfers between devices, on_device(): lax.all_to_all(send_hidden, 'ctx', split_axis=0, concat_axis=0, tiled=True)  66 us
    all_to_all x1, waiting for transfers between devices, on_device(): lax.all_to_all(send_grad, 'ctx', split_axis=0, concat_axis=0, tiled=True)  64.7 us
    all_to_all x1, waiting for transfers between devices, on_device(): lax.all_to_all(out_rows.astype(jnp.bfloat16).reshape(ctx_count, capacity,...  61.5 us
    psum x1, blocking collectives, on_device(): lax.psum(lax.psum((part_router_w, part_router_b, coef_part), 'ctx'), 'rep')  55.7 us
    psum x1, waiting for transfers between devices, on_device(): lax.psum(lax.psum((part_router_w, part_router_b, coef_part), 'ctx'), 'rep')  44.6 us
  transfers between devices with their start and end apart: 10, of which 6 were waited for; matrix products, arithmetic and copies ran while one was open for 6% of the time, Pallas kernels for 0%

profile of v1, /device:TPU:1, one launch (start us, length us, event | category | flops | bytes accessed | tf_op | source)
XLA Modules:
  0.0 1436.5 jit_solution(364385043876456273)
XLA Ops:
  16.6 13.5 all-to-all-start
  36.7 4.2 reshape.274
  40.9 11.1 all-to-all-start.1
  55.0 66.0 %all-to-all-done.1 = bf16[64,10,1536]{2,1,0:T(8,128)(2,1)} async-done(((bf16[64,10,1536]{2,1,0:T(8,128)(2,1)}), bf16[64,10,1536]{2,1,0:T(8,128)(2,1)}, u32[]{:S(2)}, u32[]{:S(2)}) %all-to-all-start.1) | async-done | bytes 1966112 | tf_op jit(solution)/shard_map/all_to_all | solution.py:108
  121.0 6.5 broadcast_in_dim.85
  127.5 10.5 all-to-all-start.2
  142.6 199.7 %all-to-all-done.2 = bf16[64,2,24,1536]{3,2,1,0:T(8,128)(2,1)} async-done(((bf16[64,2,24,1536]{3,2,1,0:T(8,128)(2,1)}), bf16[64,2,24,1536]{3,2,1,0:T(8,128)(2,1)}, u32[]{:S(2)}, u32[]{:S(2)}) %all-to-all-start.2) | async-done | bytes 9437216 | tf_op jit(solution)/shard_map/all_to_all | solution.py:100
  342.2 8.1 copy.44
  350.3 9.8 select_convert_fusion.1
  360.1 4.2 reshape.279
  364.3 11.4 all-to-all-start.3
  378.0 5.0 mul.171
  383.3 61.5 %all-to-all-done.3 = bf16[64,10,1536]{2,1,0:T(8,128)(2,1)} async-done(((bf16[64,10,1536]{2,1,0:T(8,128)(2,1)}), bf16[64,10,1536]{2,1,0:T(8,128)(2,1)}, u32[]{:S(2)}, u32[]{:S(2)}) %all-to-all-start.3) | async-done | bytes 1966112 | tf_op jit(solution)/shard_map/all_to_all | solution.py:119
  444.8 4.3 reshape.280
  464.8 4.2 reshape.283
  469.0 11.0 all-to-all-start.4
  480.0 4.2 reshape.380
  484.2 64.7 %all-to-all-done.4 = bf16[64,10,1536]{2,1,0:T(8,128)(2,1)} async-done(((bf16[64,10,1536]{2,1,0:T(8,128)(2,1)}), bf16[64,10,1536]{2,1,0:T(8,128)(2,1)}, u32[]{:S(2)}, u32[]{:S(2)}) %all-to-all-start.4) | async-done | bytes 1966112 | tf_op jit(solution)/shard_map/all_to_all | solution.py:109
  553.6 4.0 copy.46
  557.6 9.7 convolution_bitcast_fusion
  567.3 10.7 all-to-all-start.6
  579.4 559.0 %all-reduce.9.cloned.1.call-done = f32[2880,32]{0,1:T(8,128)} async-done(((f32[2880,32]{0,1:T(8,128)}), f32[2880,32]{0,1:T(8,128)}) %all-reduce.9.cloned.1.call-update) | async-done | bytes 368656 | tf_op jit(solution)/shard_map/psum | solution.py:188
  1138.5 5.2 reduce_sum.102
  1146.7 6.3 broadcast_multiply_fusion
  1154.6 9.6 select_convert_fusion
  1164.2 4.2 reshape.285
  1168.4 5.9 all-to-all-start.5
  1178.7 44.6 %all-reduce.11.cloned.1.call-done = f32[2880,32]{0,1:T(8,128)} async-done(((f32[2880,32]{0,1:T(8,128)}), f32[2880,32]{0,1:T(8,128)}) %all-reduce.11.cloned.1.call-update) | async-done | bytes 368656 | tf_op jit(solution)/shard_map/psum | solution.py:187
  1225.1 4.2 reshape.286
  1233.9 3.8 reshape.287
  1237.8 133.3 %all-reduce.4 = (f32[32]{0:T(128)S(1)}, f32[32]{0:T(128)S(1)}) all-reduce(f32[32]{0:T(128)S(1)} %get-tuple-element.7, f32[32]{0:T(128)S(1)} %get-tuple-element.18), channel_id=1, replica_groups=mesh['ctx'=64,'rep'=4] {'ctx'}, use_global_device_ids=true, to_apply=%region_15.16 | all-reduce | flops 64 | bytes 512 | tf_op jit(solution)/shard_map/psum | solution.py:188
  1371.1 55.7 %all-reduce.5 = (f32[32]{0:T(128)S(1)}, f32[32]{0:T(128)S(1)}) all-reduce(f32[32]{0:T(128)S(1)} %get-tuple-element.9, f32[32]{0:T(128)S(1)} %get-tuple-element.10), channel_id=1, replica_groups=mesh['ctx'=64,'rep'=4] {'rep'}, use_global_device_ids=true, to_apply=%region_16.17 | all-reduce | flops 64 | bytes 512 | tf_op jit(solution)/shard_map/psum | solution.py:187
  (113 shorter events, 66.0 us)
Async XLA Ops:
  7.2 375.8 %copy-start = (bf16[1,128,2880]{1,2,0:T(8,128)(2,1)S(1)}, bf16[1,128,2880]{1,2,0:T(8,128)(2,1)}, u32[]{:S(2)}) copy-start(bf16[1,128,2880]{1,2,0:T(8,128)(2,1)} %param.9) | copy-start | bytes 2211844
  10.0 20.2 %copy-start.7 = (bf16[1,128,4,1536]{3,2,1,0:T(4,128)(2,1)S(1)}, bf16[1,128,4,1536]{3,2,1,0:T(4,128)(2,1)}, u32[]{:S(2)}) copy-start(bf16[1,128,4,1536]{3,2,1,0:T(4,128)(2,1)} %param.12) | copy-start | bytes 4718596
  16.6 24.2 %all-to-all-start = ((s32[64,1,10]{2,1,0:T(1,128)}), s32[64,1,10]{2,1,0:T(1,128)S(1)}, u32[]{:S(2)}, u32[]{:S(2)}) async-start(s32[64,1,10]{2,1,0:T(1,128)} %bitcast.5), calls=%async_computation | async-start | bytes 65536 | tf_op jit(solution)/shard_map/all_to_all | solution.py:110
  40.9 11.1 copy-start.12
  40.9 12.0 copy-start.2
  40.9 80.1 %all-to-all-start.1 = ((bf16[64,10,1536]{2,1,0:T(8,128)(2,1)}), bf16[64,10,1536]{2,1,0:T(8,128)(2,1)}, u32[]{:S(2)}, u32[]{:S(2)}) async-start(bf16[64,10,1536]{2,1,0:T(8,128)(2,1)} %reshape.274), calls=%async_computation.1 | async-start | bytes 6291456 | tf_op jit(solution)/shard_map/all_to_all | solution.py:108
  127.5 10.5 copy-start.1
  127.5 214.8 %all-to-all-start.2 = ((bf16[64,2,24,1536]{3,2,1,0:T(8,128)(2,1)}), bf16[64,2,24,1536]{3,2,1,0:T(8,128)(2,1)}, u32[]{:S(2)}, u32[]{:S(2)}) async-start(bf16[64,2,24,1536]{3,2,1,0:T(8,128)(2,1)} %bitcast.77), calls=%async_computation.2 | async-start | bytes 18874368 | tf_op jit(solution)/shard_map/all_to_all | solution.py:100
  364.3 11.4 copy-start.9
  364.3 80.5 %all-to-all-start.3 = ((bf16[64,10,1536]{2,1,0:T(8,128)(2,1)}), bf16[64,10,1536]{2,1,0:T(8,128)(2,1)}, u32[]{:S(2)}, u32[]{:S(2)}) async-start(bf16[64,10,1536]{2,1,0:T(8,128)(2,1)} %reshape.279), calls=%async_computation.3 | async-start | bytes 6291456 | tf_op jit(solution)/shard_map/all_to_all | solution.py:119
  378.0 5.0 copy-start.8
  378.0 5.0 copy-start.13
  378.0 5.2 copy-start.11
  453.7 3.0 copy-start.10
  456.7 1.8 copy-start.5
  469.0 80.0 %all-to-all-start.4 = ((bf16[64,10,1536]{2,1,0:T(8,128)(2,1)}), bf16[64,10,1536]{2,1,0:T(8,128)(2,1)}, u32[]{:S(2)}, u32[]{:S(2)}) async-start(bf16[64,10,1536]{2,1,0:T(8,128)(2,1)} %reshape.283), calls=%async_computation.4 | async-start | bytes 6291456 | tf_op jit(solution)/shard_map/all_to_all | solution.py:109
  551.9 5.7 copy-start.3
  567.3 571.2 %all-to-all-start.6 = ((f32[1,64,24,1536]{3,2,0,1:T(8,128)}), f32[1,64,24,1536]{3,2,0,1:T(8,128)}, u32[]{:S(2)}, u32[]{:S(2)}) async-start(f32[1,64,24,1536]{3,2,0,1:T(8,128)} %convolution_bitcast_fusion), calls=%async_computation.6 | async-start | bytes 18874368 | tf_op jit(solution)/shard_map/all_to_all | solution.py:167
  578.0 560.4 %all-reduce.9.cloned.1.call-start = ((), (), s32[]{:S(2)}) async-start(), calls=%async_computation.8 | async-start | bytes 753664 | tf_op jit(solution)/shard_map/psum | solution.py:188
  579.3 644.0 %all-reduce.11.cloned.1.call-start = ((), (), s32[]{:S(2)}) async-start(), calls=%async_computation.9 | async-start | bytes 753664 | tf_op jit(solution)/shard_map/psum | solution.py:187
  1138.4 288.9 %reduce-scatter.2.cloned.1.call-start = ((), (), s32[]{:S(2)}) async-start(), calls=%async_computation.10 | async-start | bytes 5898240 | tf_op jit(solution)/shard_map/reduce_scatter | solution.py:183
  1153.0 1.5 copy-start.4
  1168.4 7.2 copy-start.6
  1168.4 56.7 %all-to-all-start.5 = ((bf16[64,10,1536]{2,1,0:T(8,128)(2,1)}), bf16[64,10,1536]{2,1,0:T(8,128)(2,1)}, u32[]{:S(2)}, u32[]{:S(2)}) async-start(bf16[64,10,1536]{2,1,0:T(8,128)(2,1)} %reshape.285), calls=%async_computation.5 | async-start | bytes 6291456 | tf_op jit(solution)/shard_map/all_to_all | solution.py:126
Sparse Core Ops, SparseCore 0:
  582.0 556.3 all-reduce.8
  1141.0 82.2 all-reduce.10
  1226.1 62.7 reduce-scatter.1
